TPU v7x, 512 devices: a whole 4x4x16 slice. The times are simulated.
512 devices in a mesh: tiles: 128 (over y, z, core), samp: 4 (over x).
Axes of the slice: x: 4, y: 4, z: 16, core: 2. Of those that a mesh axis runs over, the one named last changes fastest.
Arguments:
- samples: bfloat16 [256, 131072], P('samp', 'tiles'), may hold values from -6 to 6
- omega: float32 [1280, 512, 512], P('tiles', 'samp'), may hold values from -1 to 2, as said below
- coords: int32 [1280, 2], P('tiles'), may hold values from 0 to 255, as said below
Outputs:
- updated: float32 [1280, 512, 512], P('tiles', 'samp')
Inputs may be any that keep to these rules, and one draw needn't show every extreme that they name: `coords`: tile k lies with index k // 10 of tiles. Write d for that index, and blocks d * 2 to (d + 1) * 2 - 1 as its own blocks; indices of devices wrap around. The first 2 tiles of d are the diagonal tiles (I, I) of its own blocks in order. Each other tile of d is (I, J) with I an own block and J a block of d + 1, or I a block of d - 1 and J a block of d + 1, or I < J both own blocks. No unordered pair of blocks appears twice in the whole list. `omega`: tiles with I == J are symmetric with diagonal entries from 0.5 to 2.
All inputs are finite; a program needn't handle non-finite values.
Results may differ from a plain program's by a relative error of at most 0.0023.
Values may be sent and summed in bfloat16 or wider, within the bound.
No kernel may reach another device: no remote copies, remote signals or barrier semaphores. Data moves between devices by JAX's collectives and lax.ppermute only.
A program may use at most 64 MiB of HBM per device.

v0:
```python
import jax
import jax.numpy as jnp
from jax import lax
from jax.sharding import PartitionSpec as P

BLK_DEV = 2
ITERS = 2
step_size = 0.25
penalty = 0.2


def with_halo(shard, sides, width):
    for axis, dim in sides:
        size, length = (lax.axis_size(axis), shard.shape[dim])
        up = [(i, (i + 1) % size) for i in range(size)]
        down = [(j, i) for i, j in up]
        last = lax.slice_in_dim(shard, length - width, length, axis=dim)
        leading = lax.slice_in_dim(shard, 0, width, axis=dim)
        before = lax.ppermute(last, axis, up)
        after = lax.ppermute(leading, axis, down)
        shard = jnp.concatenate([before, shard, after], axis=dim)
    return shard


def columns(matrix, start, count):
    return lax.dynamic_slice_in_dim(matrix, start, count, 1)


def add_columns(totals, block, start):
    current = lax.dynamic_slice_in_dim(totals, start, block.shape[1], 1)
    return lax.dynamic_update_slice_in_dim(totals, current + block, start, 1)


def shards(samples, omega, coords):
    quarter = lax.axis_index("samp")
    tile_rows = omega.shape[1]
    width = omega.shape[2]
    own_width = samples.shape[1]
    blocks_all = BLK_DEV * lax.axis_size("tiles")
    first_block = (lax.axis_index("tiles") - 1) * BLK_DEV
    local = (coords - first_block + blocks_all) % blocks_all
    off_diagonal = (coords[:, 0] != coords[:, 1]).astype(jnp.float32)
    offset = quarter * tile_rows
    full_rows = lax.all_gather(samples, "samp", axis=0, tiled=True)
    sample_win = with_halo(full_rows, (("tiles", 1),), own_width)
    count = sample_win.shape[0]
    row_ids = offset + lax.broadcasted_iota(jnp.int32, (tile_rows, width), 0)
    col_ids = lax.broadcasted_iota(jnp.int32, (tile_rows, width), 1)
    diagonal_cells = row_ids == col_ids
    contract_cols = (((1,), (1,)), ((), ()))
    contract_rows = (((0,), (0,)), ((), ()))
    for iteration in range(ITERS):
        omega_low = omega.astype(jnp.bfloat16)
        totals = jnp.zeros((count, 3 * own_width), jnp.float32)
        for tile_slot in range(omega.shape[0]):
            row_start = local[tile_slot, 0] * width
            col_start = local[tile_slot, 1] * width
            rows_low = omega_low[tile_slot]
            row_part = columns(sample_win, row_start + offset, tile_rows)
            col_block = columns(sample_win, col_start, width)
            to_col = jnp.dot(row_part, rows_low, preferred_element_type=jnp.float32)
            to_row = lax.dot_general(
                col_block, rows_low, contract_cols, preferred_element_type=jnp.float32
            )
            totals = add_columns(totals, to_col, col_start)
            totals = add_columns(totals, to_row * off_diagonal[tile_slot], row_start + offset)
        returned = with_halo(totals, (("tiles", 1),), own_width)
        partial_value = (
            totals[:, own_width : 2 * own_width]
            + returned[:, :own_width]
            + returned[:, 4 * own_width :]
        )
        summed = lax.psum(partial_value, "samp")
        product_own = summed.astype(jnp.bfloat16)
        product_win = with_halo(product_own, (("tiles", 1),), own_width)
        new_tiles = []
        for tile_slot in range(omega.shape[0]):
            row_start = local[tile_slot, 0] * width
            col_start = local[tile_slot, 1] * width
            product_rows = columns(product_win, row_start + offset, tile_rows)
            sample_rows = columns(sample_win, row_start + offset, tile_rows)
            sample_cols = columns(sample_win, col_start, width)
            product_cols = columns(product_win, col_start, width)
            first = lax.dot_general(
                product_rows, sample_cols, contract_rows, preferred_element_type=jnp.float32
            )
            second = lax.dot_general(
                sample_rows, product_cols, contract_rows, preferred_element_type=jnp.float32
            )
            grad = (first + second) / (2.0 * count)
            value = omega[tile_slot] - step_size * grad
            shrunk = jnp.sign(value) * jnp.maximum(jnp.abs(value) - step_size * penalty, 0.0)
            positive = 0.5 * (value + jnp.sqrt(value * value + 4.0 * step_size))
            same_block = coords[tile_slot, 0] == coords[tile_slot, 1]
            new_tiles.append(jnp.where(diagonal_cells & same_block, positive, shrunk))
        omega = jnp.stack(new_tiles)
    return omega


def solution(mesh):
    in_specs = (P("samp", "tiles"), P("tiles", "samp", None), P("tiles", None))
    out_specs = P("tiles", "samp", None)
    return jax.shard_map(shards, mesh=mesh, in_specs=in_specs, out_specs=out_specs, check_vma=False)
```

profile of v0, /device:TPU:4, one launch (start us, length us, event | category | flops | bytes accessed | tf_op | source)
XLA Modules:
  0.0 228.5 jit_solution(8097895202772696019)
XLA Ops:
  0.0 16.8 %all_gather.3 = bf16[256,1024]{1,0:T(8,128)(2,1)S(1)} all-gather(bf16[64,1024]{1,0:T(8,128)(2,1)} %param.3), channel_id=1, replica_groups=mesh['tiles'=128,'samp'=4] {'samp'}, dimensions={0}, use_global_device_ids=true | all-gather | bytes 655360 | tf_op jit(solution)/shard_map/all_gather | solution.py:44
  16.8 1.9 collective-permute-start
  18.7 7.0 %collective-permute-start.1 = (bf16[256,1024]{1,0:T(8,128)(2,1)S(1)}, bf16[256,1024]{1,0:T(8,128)(2,1)}, u32[]{:S(2)}, u32[]{:S(2)}) collective-permute-start(bf16[256,1024]{1,0:T(8,128)(2,1)S(1)} %all_gather.3), channel_id=1, source_target_pairs={{4,0},{8,4},{12,8},{16,12},{20,16},{24,20},{28,24},{32,28},{36,32}... | collective-permute-start | bytes 1572872 | tf_op jit(solution)/shard_map/ppermute | solution.py:20
  40.3 1.9 convert_element_type.14
  43.1 1.1 constant_dynamic-update-slice_fusion.2
  44.2 1.1 constant_dynamic-update-slice_fusion
  45.9 0.9 add_dynamic-update-slice_fusion.19
  49.1 0.9 add_dynamic-update-slice_fusion.17
  51.2 0.9 add_dynamic-update-slice_fusion.15
  55.5 0.9 add_dynamic-update-slice_fusion.11
  56.7 1.9 collective-permute-start.2
  58.6 7.0 %collective-permute-start.3 = (f32[256,1024]{1,0:T(8,128)S(1)}, f32[256,1024]{1,0:T(8,128)S(1)}, u32[]{:S(2)}, u32[]{:S(2)}) collective-permute-start(f32[256,1024]{1,0:T(8,128)S(1)} %get-tuple-element.8), channel_id=1, source_target_pairs={{4,0},{8,4},{12,8},{16,12},{20,16},{24,20},{28,24},{32,28},{36,32}... | collective-permute-start | bytes 3145736 | tf_op jit(solution)/shard_map/ppermute | solution.py:20
  65.6 10.5 %collective-permute-done.2 = f32[256,1024]{1,0:T(8,128)S(1)} collective-permute-done((f32[256,1024]{1,0:T(8,128)S(1)}, f32[256,1024]{1,0:T(8,128)S(1)}, u32[]{:S(2)}, u32[]{:S(2)}) %collective-permute-start.2) | collective-permute-done | bytes 1048608 | tf_op jit(solution)/shard_map/ppermute | solution.py:19
  76.1 1.8 collective-permute-done.3
  78.2 28.7 %all-reduce.2 = bf16[256,1024]{1,0:T(8,128)(2,1)S(1)} all-reduce(f32[256,1024]{1,0:T(8,128)S(1)} %fusion.61), channel_id=1, replica_groups=mesh['tiles'=128,'samp'=4] {'samp'}, use_global_device_ids=true, to_apply=%region_0.1 | all-reduce | flops 262144 | bytes 1572864 | tf_op jit(solution)/shard_map/psum | solution.py:73
  106.9 1.9 collective-permute-start.4
  108.8 7.1 %collective-permute-start.5 = (bf16[256,1024]{1,0:T(8,128)(2,1)S(1)}, bf16[256,1024]{1,0:T(8,128)(2,1)S(1)}, u32[]{:S(2)}, u32[]{:S(2)}) collective-permute-start(bf16[256,1024]{1,0:T(8,128)(2,1)S(1)} %all-reduce.2), channel_id=1, source_target_pairs={{4,0},{8,4},{12,8},{16,12},{20,16},{24,20},{28,24},{32,28},{36,32}... | collective-permute-start | bytes 1572872 | tf_op jit(solution)/shard_map/ppermute | solution.py:20
  133.9 0.9 add_dynamic-update-slice_fusion.10
  138.7 0.9 add_dynamic-update-slice_fusion.8
  141.9 0.9 add_dynamic-update-slice_fusion.6
  148.8 0.9 add_dynamic-update-slice_fusion.2
  149.9 1.9 collective-permute-start.6
  151.9 7.0 %collective-permute-start.7 = (f32[256,1024]{1,0:T(8,128)S(1)}, f32[256,1024]{1,0:T(8,128)S(1)}, u32[]{:S(2)}, u32[]{:S(2)}) collective-permute-start(f32[256,1024]{1,0:T(8,128)S(1)} %get-tuple-element.6), channel_id=1, source_target_pairs={{4,0},{8,4},{12,8},{16,12},{20,16},{24,20},{28,24},{32,28},{36,32}... | collective-permute-start | bytes 3145736 | tf_op jit(solution)/shard_map/ppermute | solution.py:20
  158.8 10.5 %collective-permute-done.6 = f32[256,1024]{1,0:T(8,128)S(1)} collective-permute-done((f32[256,1024]{1,0:T(8,128)S(1)}, f32[256,1024]{1,0:T(8,128)S(1)}, u32[]{:S(2)}, u32[]{:S(2)}) %collective-permute-start.6) | collective-permute-done | bytes 1048608 | tf_op jit(solution)/shard_map/ppermute | solution.py:19
  169.4 1.8 collective-permute-done.7
  171.4 31.7 %all-reduce.3 = bf16[256,1024]{1,0:T(8,128)(2,1)S(1)} all-reduce(f32[256,1024]{1,0:T(8,128)S(1)} %fusion.60), channel_id=1, replica_groups=mesh['tiles'=128,'samp'=4] {'samp'}, use_global_device_ids=true, to_apply=%region_1.2 | all-reduce | flops 262144 | bytes 1572864 | tf_op jit(solution)/shard_map/psum | solution.py:73
  203.1 1.9 collective-permute-start.8
  205.1 7.2 %collective-permute-start.9 = (bf16[256,1024]{1,0:T(8,128)(2,1)S(1)}, bf16[256,1024]{1,0:T(8,128)(2,1)S(1)}, u32[]{:S(2)}, u32[]{:S(2)}) collective-permute-start(bf16[256,1024]{1,0:T(8,128)(2,1)S(1)} %all-reduce.3), channel_id=1, source_target_pairs={{4,0},{8,4},{12,8},{16,12},{20,16},{24,20},{28,24},{32,28},{36,32}... | collective-permute-start | bytes 1572872 | tf_op jit(solution)/shard_map/ppermute | solution.py:20
  212.2 4.7 %collective-permute-done.8 = bf16[256,1024]{1,0:T(8,128)(2,1)S(1)} collective-permute-done((bf16[256,1024]{1,0:T(8,128)(2,1)S(1)}, bf16[256,1024]{1,0:T(8,128)(2,1)S(1)}, u32[]{:S(2)}, u32[]{:S(2)}) %collective-permute-start.8) | collective-permute-done | bytes 524320 | tf_op jit(solution)/shard_map/ppermute | solution.py:19
  216.9 1.8 collective-permute-done.9
  225.8 1.5 copy-done.20
  227.3 1.2 bitcast_dynamic-update-slice_fusion
  (133 shorter events, 35.2 us)
Async XLA Ops:
  16.8 26.3 %collective-permute-start = (bf16[256,1024]{1,0:T(8,128)(2,1)S(1)}, bf16[256,1024]{1,0:T(8,128)(2,1)}, u32[]{:S(2)}, u32[]{:S(2)}) collective-permute-start(bf16[256,1024]{1,0:T(8,128)(2,1)S(1)} %all_gather.3), channel_id=1, source_target_pairs={{0,4},{4,8},{8,12},{12,16},{16,20},{20,24},{24,28},{28,32},{32,36}... | collective-permute-start | bytes 1572872 | tf_op jit(solution)/shard_map/ppermute | solution.py:19
  18.7 25.5 %collective-permute-start.1 = (bf16[256,1024]{1,0:T(8,128)(2,1)S(1)}, bf16[256,1024]{1,0:T(8,128)(2,1)}, u32[]{:S(2)}, u32[]{:S(2)}) collective-permute-start(bf16[256,1024]{1,0:T(8,128)(2,1)S(1)} %all_gather.3), channel_id=1, source_target_pairs={{4,0},{8,4},{12,8},{16,12},{20,16},{24,20},{28,24},{32,28},{36,32}... | collective-permute-start | bytes 1572872 | tf_op jit(solution)/shard_map/ppermute | solution.py:20
  40.3 2.1 copy-start.19
  56.7 19.4 %collective-permute-start.2 = (f32[256,1024]{1,0:T(8,128)S(1)}, f32[256,1024]{1,0:T(8,128)S(1)}, u32[]{:S(2)}, u32[]{:S(2)}) collective-permute-start(f32[256,1024]{1,0:T(8,128)S(1)} %get-tuple-element.7), channel_id=1, source_target_pairs={{0,4},{4,8},{8,12},{12,16},{16,20},{20,24},{24,28},{28,32},{32,36}... | collective-permute-start | bytes 3145736 | tf_op jit(solution)/shard_map/ppermute | solution.py:19
  58.6 19.3 %collective-permute-start.3 = (f32[256,1024]{1,0:T(8,128)S(1)}, f32[256,1024]{1,0:T(8,128)S(1)}, u32[]{:S(2)}, u32[]{:S(2)}) collective-permute-start(f32[256,1024]{1,0:T(8,128)S(1)} %get-tuple-element.8), channel_id=1, source_target_pairs={{4,0},{8,4},{12,8},{16,12},{20,16},{24,20},{28,24},{32,28},{36,32}... | collective-permute-start | bytes 3145736 | tf_op jit(solution)/shard_map/ppermute | solution.py:20
  106.9 22.9 %collective-permute-start.4 = (bf16[256,1024]{1,0:T(8,128)(2,1)S(1)}, bf16[256,1024]{1,0:T(8,128)(2,1)S(1)}, u32[]{:S(2)}, u32[]{:S(2)}) collective-permute-start(bf16[256,1024]{1,0:T(8,128)(2,1)S(1)} %all-reduce.2), channel_id=1, source_target_pairs={{0,4},{4,8},{8,12},{12,16},{16,20},{20,24},{24,28},{28,32},{32,36}... | collective-permute-start | bytes 1572872 | tf_op jit(solution)/shard_map/ppermute | solution.py:19
  108.8 21.0 %collective-permute-start.5 = (bf16[256,1024]{1,0:T(8,128)(2,1)S(1)}, bf16[256,1024]{1,0:T(8,128)(2,1)S(1)}, u32[]{:S(2)}, u32[]{:S(2)}) collective-permute-start(bf16[256,1024]{1,0:T(8,128)(2,1)S(1)} %all-reduce.2), channel_id=1, source_target_pairs={{4,0},{8,4},{12,8},{16,12},{20,16},{24,20},{28,24},{32,28},{36,32}... | collective-permute-start | bytes 1572872 | tf_op jit(solution)/shard_map/ppermute | solution.py:20
  131.1 1.7 copy-start
  135.2 1.6 copy-start.3
  136.9 1.5 copy-start.5
  138.4 1.7 copy-start.7
  140.1 1.5 copy-start.9
  141.6 1.7 copy-start.11
  143.3 1.6 copy-start.13
  144.9 1.5 copy-start.15
  146.5 1.6 copy-start.17
  148.1 0.7 copy-start.1
  149.9 19.4 %collective-permute-start.6 = (f32[256,1024]{1,0:T(8,128)S(1)}, f32[256,1024]{1,0:T(8,128)S(1)}, u32[]{:S(2)}, u32[]{:S(2)}) collective-permute-start(f32[256,1024]{1,0:T(8,128)S(1)} %get-tuple-element.5), channel_id=1, source_target_pairs={{0,4},{4,8},{8,12},{12,16},{16,20},{20,24},{24,28},{28,32},{32,36}... | collective-permute-start | bytes 3145736 | tf_op jit(solution)/shard_map/ppermute | solution.py:19
  151.9 19.3 %collective-permute-start.7 = (f32[256,1024]{1,0:T(8,128)S(1)}, f32[256,1024]{1,0:T(8,128)S(1)}, u32[]{:S(2)}, u32[]{:S(2)}) collective-permute-start(f32[256,1024]{1,0:T(8,128)S(1)} %get-tuple-element.6), channel_id=1, source_target_pairs={{4,0},{8,4},{12,8},{16,12},{20,16},{24,20},{28,24},{32,28},{36,32}... | collective-permute-start | bytes 3145736 | tf_op jit(solution)/shard_map/ppermute | solution.py:20
  203.1 13.8 %collective-permute-start.8 = (bf16[256,1024]{1,0:T(8,128)(2,1)S(1)}, bf16[256,1024]{1,0:T(8,128)(2,1)S(1)}, u32[]{:S(2)}, u32[]{:S(2)}) collective-permute-start(bf16[256,1024]{1,0:T(8,128)(2,1)S(1)} %all-reduce.3), channel_id=1, source_target_pairs={{0,4},{4,8},{8,12},{12,16},{16,20},{20,24},{24,28},{28,32},{32,36}... | collective-permute-start | bytes 1572872 | tf_op jit(solution)/shard_map/ppermute | solution.py:19
  205.1 13.6 %collective-permute-start.9 = (bf16[256,1024]{1,0:T(8,128)(2,1)S(1)}, bf16[256,1024]{1,0:T(8,128)(2,1)S(1)}, u32[]{:S(2)}, u32[]{:S(2)}) collective-permute-start(bf16[256,1024]{1,0:T(8,128)(2,1)S(1)} %all-reduce.3), channel_id=1, source_target_pairs={{4,0},{8,4},{12,8},{16,12},{20,16},{24,20},{28,24},{32,28},{36,32}... | collective-permute-start | bytes 1572872 | tf_op jit(solution)/shard_map/ppermute | solution.py:20
  220.4 1.2 copy-start.4
  220.9 1.3 copy-start.6
  221.6 1.0 copy-start.8
  222.1 1.0 copy-start.10
  222.7 1.0 copy-start.12
  223.2 1.0 copy-start.14
  223.7 1.0 copy-start.16
  224.2 1.0 copy-start.18
  224.8 2.5 %copy-start.2 = (f32[128,512]{1,0:T(8,128)S(1)}, f32[128,512]{1,0:T(8,128)}, u32[]{:S(2)}) copy-start(f32[128,512]{1,0:T(8,128)} %copy-done.1) | copy-start | bytes 786436
  225.8 1.5 copy-start.20
where the time goes:
time: 230 us; the launch traced here: 228 us
  blocking collectives  77.2 us (34%)
  starting transfers between devices  44.8 us (19%)
  matrix products  36.4 us (16%)
  waiting for transfers between devices  31.1 us (14%)
  between operations  26.3 us (11%)
  local copies, waits for them, and re-layouts  9.34 us (4%)
  other arithmetic  3.42 us (1%)
    psum x2, blocking collectives, shards(): summed = lax.psum(partial_value, 'samp')  60.4 us
    ppermute x5, starting transfers between devices, with_halo(): after = lax.ppermute(leading, axis, down)  35.2 us
    ppermute x5, waiting for transfers between devices, with_halo(): before = lax.ppermute(last, axis, up)  25.8 us
    dot_general x20, matrix products, shards(): lax.dot_general(col_block, rows_low, contract_cols, preferred_element_typ...  17 us
    all_gather x1, blocking collectives, shards(): full_rows = lax.all_gather(samples, 'samp', axis=0, tiled=True)  16.8 us
    dot_general x20, matrix products, shards(): lax.dot_general(product_rows, sample_cols, contract_rows, preferred_eleme...  10.6 us
    ppermute x5, starting transfers between devices, with_halo(): before = lax.ppermute(last, axis, up)  9.59 us
    ppermute x5, waiting for transfers between devices, with_halo(): after = lax.ppermute(leading, axis, down)  5.27 us
  transfers between devices with their start and end apart: 10, of which 6 were waited for; matrix products, arithmetic and copies ran while one was open for 3% of the time, Pallas kernels for 0%

commit v1 on v0

--- a/solution.py
+++ b/solution.py
@@ -41,7 +41,10 @@
     local = (coords - first_block + blocks_all) % blocks_all
     off_diagonal = (coords[:, 0] != coords[:, 1]).astype(jnp.float32)
     offset = quarter * tile_rows
-    full_rows = lax.all_gather(samples, "samp", axis=0, tiled=True)
+    devices = lax.axis_size("samp")
+    shards_2 = jnp.stack([samples for _ in range(devices)])
+    shards_2 = lax.all_to_all(shards_2, "samp", split_axis=0, concat_axis=0)
+    full_rows = jnp.concatenate(shards_2, axis=0)
     sample_win = with_halo(full_rows, (("tiles", 1),), own_width)
     count = sample_win.shape[0]
     row_ids = offset + lax.broadcasted_iota(jnp.int32, (tile_rows, width), 0)

time: 230 us -> 231 us (level)
  blocking collectives: 77.2 us -> 60.8 us
  starting transfers between devices: 44.8 us -> 56.2 us
  waiting for transfers between devices: 31.1 us -> 36.2 us
    all_gather x1 -> x0, blocking collectives: 16.8 us -> none  [shards(): full_rows = lax.all_gather(samples, 'samp', axis=0, tiled=True)]
    all_to_all x0 -> x1, starting transfers between devices: none -> 9.29 us  [shards(): shards_2 = lax.all_to_all(shards_2, 'samp', split_axis=0, concat_axis=0)]
    all_to_all x0 -> x1, waiting for transfers between devices: none -> 5.12 us  [shards(): shards_2 = lax.all_to_all(shards_2, 'samp', split_axis=0, concat_axis=0)]
  transfers between devices with their start and end apart: 10 -> 11, of which waited for: 6 -> 7; matrix products, arithmetic and copies ran while one was open for 3% -> 2% of each run, Pallas kernels for 0% -> 0%
where the time goes in v1:
time: 231 us; the launch traced here: 230 us
  blocking collectives  60.8 us (26%)
  starting transfers between devices  56.2 us (24%)
  matrix products  36.4 us (16%)
  waiting for transfers between devices  36.2 us (16%)
  between operations  26.3 us (11%)
  local copies, waits for them, and re-layouts  9.64 us (4%)
  other arithmetic  4.04 us (2%)
    psum x2, blocking collectives, shards(): summed = lax.psum(partial_value, 'samp')  60.8 us
    ppermute x5, starting transfers between devices, with_halo(): after = lax.ppermute(leading, axis, down)  37.3 us
    ppermute x5, waiting for transfers between devices, with_halo(): before = lax.ppermute(last, axis, up)  25.8 us
    dot_general x20, matrix products, shards(): lax.dot_general(col_block, rows_low, contract_cols, preferred_element_typ...  17 us
    dot_general x20, matrix products, shards(): lax.dot_general(product_rows, sample_cols, contract_rows, preferred_eleme...  10.6 us
    ppermute x5, starting transfers between devices, with_halo(): before = lax.ppermute(last, axis, up)  9.59 us
    all_to_all x1, starting transfers between devices, shards(): shards_2 = lax.all_to_all(shards_2, 'samp', split_axis=0, concat_axis=0)  9.29 us
    ppermute x5, waiting for transfers between devices, with_halo(): after = lax.ppermute(leading, axis, down)  5.27 us
  transfers between devices with their start and end apart: 11, of which 7 were waited for; matrix products, arithmetic and copies ran while one was open for 2% of the time, Pallas kernels for 0%

profile of v1, /device:TPU:4, one launch (start us, length us, event | category | flops | bytes accessed | tf_op | source)
XLA Modules:
  0.0 229.6 jit_solution(14488314306919562)
XLA Ops:
  0.0 1.8 stack.62
  1.8 9.3 %all-to-all-start = ((bf16[4,64,1024]{2,1,0:T(8,128)(2,1)}), bf16[4,64,1024]{2,1,0:T(8,128)(2,1)S(1)}, u32[]{:S(2)}, u32[]{:S(2)}) async-start(bf16[4,64,1024]{2,1,0:T(8,128)(2,1)} %stack.62), calls=%async_computation | async-start | bytes 1048576 | tf_op jit(solution)/shard_map/all_to_all | solution.py:46
  11.1 5.1 %all-to-all-done = bf16[4,64,1024]{2,1,0:T(8,128)(2,1)S(1)} async-done(((bf16[4,64,1024]{2,1,0:T(8,128)(2,1)}), bf16[4,64,1024]{2,1,0:T(8,128)(2,1)S(1)}, u32[]{:S(2)}, u32[]{:S(2)}) %all-to-all-start) | async-done | bytes 524320 | tf_op jit(solution)/shard_map/all_to_all | solution.py:46
  16.2 1.9 collective-permute-start
  18.1 9.1 %collective-permute-start.1 = (bf16[256,1024]{1,0:T(8,128)(2,1)S(1)}, bf16[256,1024]{1,0:T(8,128)(2,1)}, u32[]{:S(2)}, u32[]{:S(2)}) collective-permute-start(bf16[256,1024]{1,0:T(8,128)(2,1)S(1)} %bitcast.162), channel_id=1, source_target_pairs={{4,0},{8,4},{12,8},{16,12},{20,16},{24,20},{28,24},{32,28},{36,32}... | collective-permute-start | bytes 1572872 | tf_op jit(solution)/shard_map/ppermute | solution.py:20
  41.1 1.9 convert_element_type.14
  44.7 1.3 pad_maximum_fusion
  47.7 0.9 fusion.59
  53.1 0.9 add_dynamic-update-slice_fusion.14
  55.2 0.9 add_dynamic-update-slice_fusion.12
  57.4 1.9 collective-permute-start.2
  59.3 7.0 %collective-permute-start.3 = (f32[256,1024]{1,0:T(8,128)S(1)}, f32[256,1024]{1,0:T(8,128)S(1)}, u32[]{:S(2)}, u32[]{:S(2)}) collective-permute-start(f32[256,1024]{1,0:T(8,128)S(1)} %get-tuple-element.8), channel_id=1, source_target_pairs={{4,0},{8,4},{12,8},{16,12},{20,16},{24,20},{28,24},{32,28},{36,32}... | collective-permute-start | bytes 3145736 | tf_op jit(solution)/shard_map/ppermute | solution.py:20
  66.3 10.5 %collective-permute-done.2 = f32[256,1024]{1,0:T(8,128)S(1)} collective-permute-done((f32[256,1024]{1,0:T(8,128)S(1)}, f32[256,1024]{1,0:T(8,128)S(1)}, u32[]{:S(2)}, u32[]{:S(2)}) %collective-permute-start.2) | collective-permute-done | bytes 1048608 | tf_op jit(solution)/shard_map/ppermute | solution.py:19
  76.8 1.8 collective-permute-done.3
  78.9 30.5 %all-reduce.2 = bf16[256,1024]{1,0:T(8,128)(2,1)S(1)} all-reduce(f32[256,1024]{1,0:T(8,128)S(1)} %fusion.61), channel_id=1, replica_groups=mesh['tiles'=128,'samp'=4] {'samp'}, use_global_device_ids=true, to_apply=%region_0.1 | all-reduce | flops 262144 | bytes 1572864 | tf_op jit(solution)/shard_map/psum | solution.py:76
  109.4 1.9 collective-permute-start.4
  111.3 7.1 %collective-permute-start.5 = (bf16[256,1024]{1,0:T(8,128)(2,1)S(1)}, bf16[256,1024]{1,0:T(8,128)(2,1)S(1)}, u32[]{:S(2)}, u32[]{:S(2)}) collective-permute-start(bf16[256,1024]{1,0:T(8,128)(2,1)S(1)} %all-reduce.2), channel_id=1, source_target_pairs={{4,0},{8,4},{12,8},{16,12},{20,16},{24,20},{28,24},{32,28},{36,32}... | collective-permute-start | bytes 1572872 | tf_op jit(solution)/shard_map/ppermute | solution.py:20
  136.3 0.9 add_dynamic-update-slice_fusion.10
  137.9 0.9 fusion.57
  146.0 0.9 add_dynamic-update-slice_fusion.5
  149.2 0.9 add_dynamic-update-slice_fusion.3
  152.4 1.9 collective-permute-start.6
  154.3 7.0 %collective-permute-start.7 = (f32[256,1024]{1,0:T(8,128)S(1)}, f32[256,1024]{1,0:T(8,128)S(1)}, u32[]{:S(2)}, u32[]{:S(2)}) collective-permute-start(f32[256,1024]{1,0:T(8,128)S(1)} %get-tuple-element.6), channel_id=1, source_target_pairs={{4,0},{8,4},{12,8},{16,12},{20,16},{24,20},{28,24},{32,28},{36,32}... | collective-permute-start | bytes 3145736 | tf_op jit(solution)/shard_map/ppermute | solution.py:20
  161.3 10.5 %collective-permute-done.6 = f32[256,1024]{1,0:T(8,128)S(1)} collective-permute-done((f32[256,1024]{1,0:T(8,128)S(1)}, f32[256,1024]{1,0:T(8,128)S(1)}, u32[]{:S(2)}, u32[]{:S(2)}) %collective-permute-start.6) | collective-permute-done | bytes 1048608 | tf_op jit(solution)/shard_map/ppermute | solution.py:19
  171.8 1.8 collective-permute-done.7
  173.9 30.4 %all-reduce.3 = bf16[256,1024]{1,0:T(8,128)(2,1)S(1)} all-reduce(f32[256,1024]{1,0:T(8,128)S(1)} %fusion.60), channel_id=1, replica_groups=mesh['tiles'=128,'samp'=4] {'samp'}, use_global_device_ids=true, to_apply=%region_1.2 | all-reduce | flops 262144 | bytes 1572864 | tf_op jit(solution)/shard_map/psum | solution.py:76
  204.3 1.9 collective-permute-start.8
  206.2 7.2 %collective-permute-start.9 = (bf16[256,1024]{1,0:T(8,128)(2,1)S(1)}, bf16[256,1024]{1,0:T(8,128)(2,1)S(1)}, u32[]{:S(2)}, u32[]{:S(2)}) collective-permute-start(bf16[256,1024]{1,0:T(8,128)(2,1)S(1)} %all-reduce.3), channel_id=1, source_target_pairs={{4,0},{8,4},{12,8},{16,12},{20,16},{24,20},{28,24},{32,28},{36,32}... | collective-permute-start | bytes 1572872 | tf_op jit(solution)/shard_map/ppermute | solution.py:20
  213.4 4.7 %collective-permute-done.8 = bf16[256,1024]{1,0:T(8,128)(2,1)S(1)} collective-permute-done((bf16[256,1024]{1,0:T(8,128)(2,1)S(1)}, bf16[256,1024]{1,0:T(8,128)(2,1)S(1)}, u32[]{:S(2)}, u32[]{:S(2)}) %collective-permute-start.8) | collective-permute-done | bytes 524320 | tf_op jit(solution)/shard_map/ppermute | solution.py:19
  218.1 1.8 collective-permute-done.9
  226.9 1.5 copy-done.21
  228.4 1.2 bitcast_dynamic-update-slice_fusion
  (135 shorter events, 36.1 us)
Async XLA Ops:
  0.0 27.2 %copy-start.20 = (s32[10,2]{0,1:T(2,128)S(1)}, s32[10,2]{0,1:T(2,128)}, u32[]{:S(2)}) copy-start(s32[10,2]{0,1:T(2,128)} %param.5) | copy-start | bytes 244
  1.8 14.4 %all-to-all-start = ((bf16[4,64,1024]{2,1,0:T(8,128)(2,1)}), bf16[4,64,1024]{2,1,0:T(8,128)(2,1)S(1)}, u32[]{:S(2)}, u32[]{:S(2)}) async-start(bf16[4,64,1024]{2,1,0:T(8,128)(2,1)} %stack.62), calls=%async_computation | async-start | bytes 1048576 | tf_op jit(solution)/shard_map/all_to_all | solution.py:46
  16.2 27.7 %collective-permute-start = (bf16[256,1024]{1,0:T(8,128)(2,1)S(1)}, bf16[256,1024]{1,0:T(8,128)(2,1)S(1)}, u32[]{:S(2)}, u32[]{:S(2)}) collective-permute-start(bf16[256,1024]{1,0:T(8,128)(2,1)S(1)} %bitcast.161), channel_id=1, source_target_pairs={{0,4},{4,8},{8,12},{12,16},{16,20},{20,24},{24,28},{28,32},{32,36}... | collective-permute-start | bytes 1572872 | tf_op jit(solution)/shard_map/ppermute | solution.py:19
  18.1 26.6 %collective-permute-start.1 = (bf16[256,1024]{1,0:T(8,128)(2,1)S(1)}, bf16[256,1024]{1,0:T(8,128)(2,1)}, u32[]{:S(2)}, u32[]{:S(2)}) collective-permute-start(bf16[256,1024]{1,0:T(8,128)(2,1)S(1)} %bitcast.162), channel_id=1, source_target_pairs={{4,0},{8,4},{12,8},{16,12},{20,16},{24,20},{28,24},{32,28},{36,32}... | collective-permute-start | bytes 1572872 | tf_op jit(solution)/shard_map/ppermute | solution.py:20
  43.9 0.8 copy-start.19
  57.4 19.4 %collective-permute-start.2 = (f32[256,1024]{1,0:T(8,128)S(1)}, f32[256,1024]{1,0:T(8,128)S(1)}, u32[]{:S(2)}, u32[]{:S(2)}) collective-permute-start(f32[256,1024]{1,0:T(8,128)S(1)} %get-tuple-element.7), channel_id=1, source_target_pairs={{0,4},{4,8},{8,12},{12,16},{16,20},{20,24},{24,28},{28,32},{32,36}... | collective-permute-start | bytes 3145736 | tf_op jit(solution)/shard_map/ppermute | solution.py:19
  59.3 19.3 %collective-permute-start.3 = (f32[256,1024]{1,0:T(8,128)S(1)}, f32[256,1024]{1,0:T(8,128)S(1)}, u32[]{:S(2)}, u32[]{:S(2)}) collective-permute-start(f32[256,1024]{1,0:T(8,128)S(1)} %get-tuple-element.8), channel_id=1, source_target_pairs={{4,0},{8,4},{12,8},{16,12},{20,16},{24,20},{28,24},{32,28},{36,32}... | collective-permute-start | bytes 3145736 | tf_op jit(solution)/shard_map/ppermute | solution.py:20
  109.4 22.8 %collective-permute-start.4 = (bf16[256,1024]{1,0:T(8,128)(2,1)S(1)}, bf16[256,1024]{1,0:T(8,128)(2,1)S(1)}, u32[]{:S(2)}, u32[]{:S(2)}) collective-permute-start(bf16[256,1024]{1,0:T(8,128)(2,1)S(1)} %all-reduce.2), channel_id=1, source_target_pairs={{0,4},{4,8},{8,12},{12,16},{16,20},{20,24},{24,28},{28,32},{32,36}... | collective-permute-start | bytes 1572872 | tf_op jit(solution)/shard_map/ppermute | solution.py:19
  111.3 20.9 %collective-permute-start.5 = (bf16[256,1024]{1,0:T(8,128)(2,1)S(1)}, bf16[256,1024]{1,0:T(8,128)(2,1)S(1)}, u32[]{:S(2)}, u32[]{:S(2)}) collective-permute-start(bf16[256,1024]{1,0:T(8,128)(2,1)S(1)} %all-reduce.2), channel_id=1, source_target_pairs={{4,0},{8,4},{12,8},{16,12},{20,16},{24,20},{28,24},{32,28},{36,32}... | collective-permute-start | bytes 1572872 | tf_op jit(solution)/shard_map/ppermute | solution.py:20
  133.5 1.7 copy-start
  137.6 1.7 copy-start.3
  139.3 1.6 copy-start.5
  140.9 1.6 copy-start.7
  142.6 1.6 copy-start.9
  144.2 1.5 copy-start.11
  145.7 1.7 copy-start.13
  147.4 1.5 copy-start.15
  148.9 1.7 copy-start.17
  152.4 19.4 %collective-permute-start.6 = (f32[256,1024]{1,0:T(8,128)S(1)}, f32[256,1024]{1,0:T(8,128)S(1)}, u32[]{:S(2)}, u32[]{:S(2)}) collective-permute-start(f32[256,1024]{1,0:T(8,128)S(1)} %get-tuple-element.5), channel_id=1, source_target_pairs={{0,4},{4,8},{8,12},{12,16},{16,20},{20,24},{24,28},{28,32},{32,36}... | collective-permute-start | bytes 3145736 | tf_op jit(solution)/shard_map/ppermute | solution.py:19
  154.3 19.3 %collective-permute-start.7 = (f32[256,1024]{1,0:T(8,128)S(1)}, f32[256,1024]{1,0:T(8,128)S(1)}, u32[]{:S(2)}, u32[]{:S(2)}) collective-permute-start(f32[256,1024]{1,0:T(8,128)S(1)} %get-tuple-element.6), channel_id=1, source_target_pairs={{4,0},{8,4},{12,8},{16,12},{20,16},{24,20},{28,24},{32,28},{36,32}... | collective-permute-start | bytes 3145736 | tf_op jit(solution)/shard_map/ppermute | solution.py:20
  204.3 13.8 %collective-permute-start.8 = (bf16[256,1024]{1,0:T(8,128)(2,1)S(1)}, bf16[256,1024]{1,0:T(8,128)(2,1)S(1)}, u32[]{:S(2)}, u32[]{:S(2)}) collective-permute-start(bf16[256,1024]{1,0:T(8,128)(2,1)S(1)} %all-reduce.3), channel_id=1, source_target_pairs={{0,4},{4,8},{8,12},{12,16},{16,20},{20,24},{24,28},{28,32},{32,36}... | collective-permute-start | bytes 1572872 | tf_op jit(solution)/shard_map/ppermute | solution.py:19
  206.2 13.6 %collective-permute-start.9 = (bf16[256,1024]{1,0:T(8,128)(2,1)S(1)}, bf16[256,1024]{1,0:T(8,128)(2,1)S(1)}, u32[]{:S(2)}, u32[]{:S(2)}) collective-permute-start(bf16[256,1024]{1,0:T(8,128)(2,1)S(1)} %all-reduce.3), channel_id=1, source_target_pairs={{4,0},{8,4},{12,8},{16,12},{20,16},{24,20},{28,24},{32,28},{36,32}... | collective-permute-start | bytes 1572872 | tf_op jit(solution)/shard_map/ppermute | solution.py:20
  221.5 1.2 copy-start.4
  222.0 1.3 copy-start.6
  222.8 1.0 copy-start.8
  223.3 1.0 copy-start.10
  223.8 1.0 copy-start.12
  224.3 1.0 copy-start.14
  224.9 1.0 copy-start.16
  225.4 1.0 copy-start.18
  225.9 2.5 %copy-start.2 = (f32[128,512]{1,0:T(8,128)S(1)}, f32[128,512]{1,0:T(8,128)}, u32[]{:S(2)}) copy-start(f32[128,512]{1,0:T(8,128)} %copy-done.1) | copy-start | bytes 786436
  226.9 1.5 copy-start.21
  (1 other events, 0.7 us)
